TPU v7x, 256 devices: a whole 4x4x8 slice. The times are simulated.
256 devices in a mesh: dp: 128 (over y_hi, x, z, core), pipe: 2 (over y_lo).
Axes of the slice: x: 4, y: 4 (y_hi: 2, y_lo: 2; y = y_hi * 2 + y_lo), z: 8, core: 2. Of those that a mesh axis runs over, the one named last changes fastest.
Arguments:
- block_input: bfloat16 [2, 32768, 1536], P('pipe', 'dp'), may hold values from -100 to 100
- saved_qkv: bfloat16 [2, 32768, 4608], P('pipe', 'dp'), may hold values from -10 to 10
- cotangent: bfloat16 [2, 32768, 1536], P('pipe', 'dp'), may hold values from -6 to 6
- mod_table: float32 [2, 3, 1536], P('pipe'), may hold values from -3 to 3
- clip_condition: float32 [2, 1024, 4608], P('pipe', 'dp'), may hold values from -3 to 3
- clip_frames: int32 [2, 1024], P('pipe', 'dp'), may hold values from 0 to 8, as said below
- frame_tokens: int32 [2, 1024], P('pipe', 'dp'), may hold values from 2 to 64, as said below
- tile_layout: int32 [2, 256, 2], P('pipe', 'dp'), may hold values from 0 to 1, as said below
- frozen_qkv: bfloat16 [2, 1536, 4608], P('pipe', 'dp'), may hold values from -0.15625 to 0.15625
- frozen_out: bfloat16 [2, 1536, 1536], P('pipe', 'dp'), may hold values from -0.15625 to 0.15625
- adapters: bfloat16 [2, 9216, 128], P('pipe'), may hold values from -0.15625 to 0.15625
Outputs:
- upstream: bfloat16 [2, 32768, 1536], P('pipe', 'dp')
- d_table: float32 [2, 3, 1536], P('pipe')
- d_adapters: float32 [2, 9216, 128], P('pipe', 'dp')
Inputs may be any that keep to these rules, and one draw needn't show every extreme that they name: `clip_frames`: clips are packed in slot order; a slot with 0 frames holds no clip and so does every later slot of that device; the clips of one device hold at most 256 tokens. `frame_tokens`: even. `tile_layout`: every diagonal tile is live.
All inputs are finite; a program needn't handle non-finite values.
Results may differ from a plain program's by a relative error of at most 0.0065.
Values may be sent and summed in bfloat16 or wider, within the bound.
A program may use at most 128 MiB of HBM per device.

v0:
```python
import jax
import jax.numpy as jnp
from jax import lax
from jax.sharding import PartitionSpec as P

HEAD = 128
TILE = 128
EPSILON = 1e-06
HIGH = lax.Precision.HIGHEST


def passed_along(block, axis, distance):
    devices = range(lax.axis_size(axis))
    route = [((i - distance) % len(devices), i) for i in devices]
    return lax.ppermute(block, axis, route)


def contract_last(left, right):
    return lax.dot_general(
        left, right, (((1,), (1,)), ((), ())), preferred_element_type=jnp.float32
    )


def contract_first(left, right):
    return lax.dot_general(
        left, right, (((0,), (0,)), ((), ())), preferred_element_type=jnp.float32
    )


def on_device(
    block_input,
    saved_qkv,
    cotangent,
    mod_table,
    clip_condition,
    clip_frames,
    frame_tokens,
    tile_layout,
    frozen_qkv,
    frozen_out,
    adapters,
):
    tokens_here = block_input[0]
    rows, width = tokens_here.shape
    saved = saved_qkv[0]
    inner = saved.shape[1] // 3
    heads = inner // HEAD
    slots = clip_frames.shape[1]
    tiles = tile_layout.shape[1]
    adapter_rows = adapters[0]
    down_qkv = adapter_rows[:width]
    up_qkv = adapter_rows[width : width + 3 * inner]
    down_out = adapter_rows[width + 3 * inner : width + 4 * inner]
    up_out = adapter_rows[width + 4 * inner :]
    clip_ends = jnp.cumsum(clip_frames[0] * frame_tokens[0])
    position = jnp.arange(rows, dtype=jnp.int32)
    clip_of = jnp.sum((position[:, None] >= clip_ends[None, :]).astype(jnp.int32), axis=1)
    onehot_clip = (clip_of[:, None] == jnp.arange(slots, dtype=jnp.int32)[None, :]).astype(
        jnp.float32
    )
    modulation = mod_table[0].reshape(1, 3 * width) + jnp.dot(
        onehot_clip, clip_condition[0], precision=HIGH
    )
    shift_rows = modulation[:, :width]
    scale_rows = modulation[:, width : 2 * width]
    gate_rows = modulation[:, 2 * width :]
    inputs_f = tokens_here.astype(jnp.float32)
    centered = inputs_f - jnp.mean(inputs_f, axis=1, keepdims=True)
    inverse = lax.rsqrt(jnp.mean(centered * centered, axis=1, keepdims=True) + EPSILON)
    normed = centered * inverse
    modded = (normed * (1.0 + scale_rows) + shift_rows).astype(jnp.bfloat16)
    tile_onehot = (
        (position // TILE)[:, None] == jnp.arange(tiles, dtype=jnp.int32)[None, :]
    ).astype(jnp.float32)
    live_rows = jnp.dot(tile_onehot, tile_layout[0].astype(jnp.float32), precision=HIGH)
    live_pairs = jnp.dot(live_rows, tile_onehot.T, precision=HIGH) > 0.5
    allowed = live_pairs & (clip_of[:, None] == clip_of[None, :])
    queries = saved[:, :inner].reshape(rows, heads, HEAD)
    key_rows = saved[:, inner : 2 * inner].reshape(rows, heads, HEAD)
    value_rows = saved[:, 2 * inner :].reshape(rows, heads, HEAD)
    factor = HEAD ** (-0.5)
    scores = (
        jnp.einsum("qhd,khd->hqk", queries, key_rows, preferred_element_type=jnp.float32) * factor
    )
    scores = jnp.where(allowed[None], scores, -jnp.inf)
    probs = jax.nn.softmax(scores, axis=2)
    probs_b = probs.astype(jnp.bfloat16)
    attention = (
        jnp.einsum("hqk,khd->qhd", probs_b, value_rows, preferred_element_type=jnp.float32)
        .reshape(rows, inner)
        .astype(jnp.bfloat16)
    )
    out_whole = lax.all_gather(frozen_out[0], "dp", axis=0, tiled=True)
    low_out = jnp.dot(attention, down_out, preferred_element_type=jnp.float32).astype(jnp.bfloat16)
    branch = jnp.dot(attention, out_whole, preferred_element_type=jnp.float32) + contract_last(
        low_out, up_out
    )
    cotangent_f = cotangent[0].astype(jnp.float32)
    gated = (gate_rows * cotangent_f).astype(jnp.bfloat16)
    low_grad_out = jnp.dot(gated, up_out, preferred_element_type=jnp.float32).astype(jnp.bfloat16)
    grad_attention = (
        contract_last(gated, out_whole) + contract_last(low_grad_out, down_out)
    ).astype(jnp.bfloat16)
    grad_heads = grad_attention.reshape(rows, heads, HEAD)
    grad_probs = jnp.einsum(
        "qhd,khd->hqk", grad_heads, value_rows, preferred_element_type=jnp.float32
    )
    delta = jnp.sum(probs * grad_probs, axis=2, keepdims=True)
    grad_scores = (probs * (grad_probs - delta) * factor).astype(jnp.bfloat16)
    grad_query = jnp.einsum(
        "hqk,khd->qhd", grad_scores, key_rows, preferred_element_type=jnp.float32
    ).reshape(rows, inner)
    grad_key = jnp.einsum(
        "hqk,qhd->khd", grad_scores, queries, preferred_element_type=jnp.float32
    ).reshape(rows, inner)
    grad_value = jnp.einsum(
        "hqk,qhd->khd", probs_b, grad_heads, preferred_element_type=jnp.float32
    ).reshape(rows, inner)
    grad_qkv = jnp.concatenate([grad_query, grad_key, grad_value], axis=1).astype(jnp.bfloat16)
    low_in = jnp.dot(modded, down_qkv, preferred_element_type=jnp.float32).astype(jnp.bfloat16)
    low_grad_in = jnp.dot(grad_qkv, up_qkv, preferred_element_type=jnp.float32).astype(jnp.bfloat16)
    frozen_part = contract_last(grad_qkv, lax.all_gather(frozen_qkv[0], "dp", axis=0, tiled=True))
    grad_modded = frozen_part + contract_last(low_grad_in, down_qkv)
    grad_normed = grad_modded * (1.0 + scale_rows)
    grad_input = cotangent_f + inverse * (
        grad_normed
        - jnp.mean(grad_normed, axis=1, keepdims=True)
        - normed * jnp.mean(grad_normed * normed, axis=1, keepdims=True)
    )
    grad_input = grad_input.astype(jnp.bfloat16)
    table_part = jnp.stack(
        [
            jnp.sum(grad_modded, axis=0),
            jnp.sum(grad_modded * normed, axis=0),
            jnp.sum(cotangent_f * branch, axis=0),
        ]
    )
    adapter_part = jnp.concatenate(
        [
            contract_first(modded, low_grad_in),
            contract_first(grad_qkv, low_in),
            contract_first(attention, low_grad_out),
            contract_first(gated, low_out),
        ],
        axis=0,
    )
    replicas = lax.axis_size("dp")
    table_sum = lax.psum(table_part, "dp")
    adapter_sum = lax.psum_scatter(adapter_part, "dp", scatter_dimension=0, tiled=True)
    passed_back = passed_along(grad_input, "pipe", -1)
    return (passed_back[None], (table_sum / replicas)[None], (adapter_sum / replicas)[None])


def solution(mesh):
    placed = (
        P("pipe", "dp", None),
        P("pipe", "dp", None),
        P("pipe", "dp", None),
        P("pipe", None, None),
        P("pipe", "dp", None),
        P("pipe", "dp"),
        P("pipe", "dp"),
        P("pipe", "dp", None),
        P("pipe", "dp", None),
        P("pipe", "dp", None),
        P("pipe", None, None),
    )
    return jax.shard_map(
        on_device,
        mesh=mesh,
        in_specs=placed,
        out_specs=(P("pipe", "dp", None), P("pipe", None, None), P("pipe", "dp", None)),
        check_vma=False,
    )
```

profile of v0, /device:TPU:24, one launch (start us, length us, event | category | flops | bytes accessed | tf_op | source)
XLA Modules:
  0.0 1030.8 jit_solution(3431634579124080414)
XLA Ops:
  7.2 1.5 copy.65
  8.8 1.8 copy.72
  12.4 0.9 fusion.79
  13.9 2.9 copy.62
  17.4 1.5 fusion.92
  18.9 4.2 fusion.93
  23.1 2.3 convolution_convert_fusion
  25.4 1.7 convolution_convert_fusion.3
  27.1 2.0 convolution_add_fusion
  29.5 1.7 convolution_convert_fusion.4
  31.6 1.3 fusion.97
  33.0 111.5 %all-gather.5.cloned.1.call-done = bf16[1,1536,1536]{2,0,1:T(2,128)(2,1)} async-done(((bf16[1,12,1536]{2,0,1:T(2,128)(2,1)}), bf16[1,1536,1536]{2,0,1:T(2,128)(2,1)}) %all-gather.5.cloned.1.call-update) | async-done | bytes 4718608 | tf_op jit(solution)/shard_map/all_gather | solution.py:93
  144.5 5.4 fusion.7
  149.8 2.2 fusion.11
  152.1 2.3 copy.66
  154.4 3.4 fusion.94
  157.8 7.1 fusion.44
  164.9 6.9 fusion.47
  171.8 2.7 convolution_convert_fusion.1
  174.5 0.9 copy-done.16
  176.2 153.9 %all-gather.7.cloned.1.call-done = bf16[1,1536,4608]{2,0,1:T(2,128)(2,1)} async-done(((bf16[1,12,4608]{2,0,1:T(2,128)(2,1)}), bf16[1,1536,4608]{2,0,1:T(2,128)(2,1)}) %all-gather.7.cloned.1.call-update) | async-done | bytes 14155792 | tf_op jit(solution)/shard_map/all_gather | solution.py:122
  330.1 14.6 %fusion.2 = f32[256,1536]{1,0:T(8,128)S(1)} fusion(bf16[1,1536,4608]{2,0,1:T(2,128)(2,1)} %all-gather.7.cloned.1.call-done, bf16[256,1536]{0,1:T(8,128)(2,1)} %bitcast.145, bf16[256,1536]{0,1:T(8,128)(2,1)} %bitcast.141, bf16[256,1536]{0,1:T(8,128)(2,1)S(1)} %bitcast.140), kind=kOutput, calls=%fused_computation.2 | convolution fusion | flops 3630956544 | bytes 18087936 | tf_op jit(solution)/shard_map/dot_general | solution.py:19
  344.8 2.4 fusion.91
  347.2 3.6 fusion.35
  350.8 4.3 fusion.58
  355.5 6.9 pad_maximum_fusion
  362.4 1.1 copy-done.11
  363.6 5.2 fusion.5
  368.8 1.4 fusion.51
  370.3 651.1 %psum.7 = f32[3,1536]{1,0:T(4,128)S(1)} all-reduce(f32[3,1536]{1,0:T(4,128)S(1)} %pad_maximum_fusion.2), channel_id=1, replica_groups=mesh['dp'=128,'pipe'=2] {'dp'}, use_global_device_ids=true, to_apply=%region_12.13 | all-reduce | flops 4608 | bytes 36864 | tf_op jit(solution)/shard_map/psum | solution.py:148
  1022.0 1.4 multiply_bitcast_fusion
  1023.4 0.9 copy.97
  (64 shorter events, 5.9 us)
Async XLA Ops:
  7.2 20.0 %copy-start = (f32[1,8,4608]{2,1,0:T(8,128)S(1)}, f32[1,8,4608]{2,1,0:T(8,128)}, u32[]{:S(2)}) copy-start(f32[1,8,4608]{2,1,0:T(8,128)} %param.15) | copy-start | bytes 442372
  7.2 137.3 %all-gather.5.cloned.1.call-start = ((), (), s32[]{:S(2)}) async-start(), calls=%async_computation.1 | async-start | bytes 9510912 | tf_op jit(solution)/shard_map/all_gather | solution.py:93
  8.8 321.4 %all-gather.7.cloned.1.call-start = ((), (), s32[]{:S(2)}) async-start(), calls=%async_computation.2 | async-start | bytes 28532736 | tf_op jit(solution)/shard_map/all_gather | solution.py:122
  10.6 1011.4 %reduce-scatter.4.cloned.1.call-start = ((), (), s32[]{:S(2)}) async-start(), calls=%async_computation.3 | async-start | bytes 4755456
  13.9 2.9 copy-start.3
  18.9 4.2 copy-start.5
  25.4 5.7 copy-start.10
  27.1 2.1 copy-start.4
  29.2 2.3 copy-start.2
  29.5 2.2 copy-start.8
  164.9 6.9 copy-start.7
  171.8 3.6 copy-start.12
  171.8 3.6 copy-start.13
  171.8 3.6 copy-start.15
  174.5 0.9 copy-start.16
  175.4 154.7 %copy-start.14 = (bf16[12,256,128]{1,2,0:T(8,128)(2,1)S(1)}, bf16[12,256,128]{1,2,0:T(8,128)(2,1)}, u32[]{:S(2)}) copy-start(bf16[12,256,128]{1,2,0:T(8,128)(2,1)} %fusion.44) | copy-start | bytes 2359300
  350.8 4.7 copy-start.6
  362.4 1.1 copy-start.11
  363.6 5.2 copy-start.9
  363.6 660.8 %copy-start.1 = (f32[1,8,4608]{2,1,0:T(8,128)S(1)}, f32[1,8,4608]{2,1,0:T(8,128)}, u32[]{:S(2)}) copy-start(f32[1,8,4608]{2,1,0:T(8,128)} %param.15) | copy-start | bytes 442372
  368.7 653.3 %collective-permute-start = (bf16[256,1536]{1,0:T(8,128)(2,1)S(1)}, bf16[256,1536]{1,0:T(8,128)(2,1)S(1)}, u32[]{:S(2)}, u32[]{:S(2)}) collective-permute-start(bf16[256,1536]{1,0:T(8,128)(2,1)S(1)} %copy-done.9), channel_id=1, source_target_pairs={{1,0},{0,1},{3,2},{2,3},{5,4},{4,5},{7,6},{6,7},{9,8},{8,9},{11,10... | collective-permute-start | bytes 2359304 | tf_op jit(solution)/shard_map/ppermute | solution.py:15
Sparse Core Ops, SparseCore 0:
  11.9 132.5 all-gather.4
  148.3 181.7 all-gather.6
  362.6 268.5 reduce-scatter.3
where the time goes:
time: 1030 us
  blocking collectives  651 us (63%)
  waiting for transfers between devices  265 us (26%)
  matrix products  71.8 us (7%)
  other arithmetic  14.4 us (1%)
  between operations  14 us (1%)
  local copies, waits for them, and re-layouts  13.9 us (1%)
    psum x1, blocking collectives, on_device(): table_sum = lax.psum(table_part, 'dp')  651 us
    all_gather x1, waiting for transfers between devices, on_device(): lax.all_gather(frozen_qkv[0], 'dp', axis=0, tiled=True)  154 us
    all_gather x1, waiting for transfers between devices, on_device(): out_whole = lax.all_gather(frozen_out[0], 'dp', axis=0, tiled=True)  111 us
    dot_general x5, matrix products, contract_last(): lax.dot_general(left, right, (((1,), (1,)), ((), ())), preferred_element_...  26 us
  transfers between devices with their start and end apart: 4, of which 2 were waited for; matrix products, arithmetic and copies ran while one was open for 6% of the time, Pallas kernels for 0%

commit v1 on v0

--- a/solution.py
+++ b/solution.py
@@ -145,7 +145,7 @@
         axis=0,
     )
     replicas = lax.axis_size("dp")
-    table_sum = lax.psum(table_part, "dp")
+    table_sum = jnp.sum(lax.all_gather(table_part, "dp"), axis=0)
     adapter_sum = lax.psum_scatter(adapter_part, "dp", scatter_dimension=0, tiled=True)
     passed_back = passed_along(grad_input, "pipe", -1)
     return (passed_back[None], (table_sum / replicas)[None], (adapter_sum / replicas)[None])

time: 1030 us -> 746 us (0.72)
  blocking collectives: 651 us -> 0 us
  waiting for transfers between devices: 265 us -> 626 us
    psum x1 -> x0, blocking collectives: 651 us -> none  [on_device(): table_sum = lax.psum(table_part, 'dp')]
    unnamed x4 -> x5, waiting for transfers between devices: 0.05 us -> 271 us
    all_gather x0 -> x1, waiting for transfers between devices: none -> 71.3 us  [on_device(): table_sum = jnp.sum(lax.all_gather(table_part, 'dp'), axis=0)]
    ppermute x1, waiting for transfers between devices: 0.01 us -> 19.7 us  [passed_along(): return lax.ppermute(block, axis, route)]
  transfers between devices with their start and end apart: 4 -> 5, of which waited for: 2 -> 5; matrix products, arithmetic and copies ran while one was open for 6% -> 10% of each run, Pallas kernels for 0% -> 0%
where the time goes in v1:
time: 746 us; the launch traced here: 744 us
  waiting for transfers between devices  626 us (84%)
  matrix products  70.2 us (9%)
  other arithmetic  17.4 us (2%)
  local copies, waits for them, and re-layouts  16.7 us (2%)
  between operations  14 us (2%)
    unnamed x5, waiting for transfers between devices  271 us
    all_gather x1, waiting for transfers between devices, on_device(): lax.all_gather(frozen_qkv[0], 'dp', axis=0, tiled=True)  153 us
    all_gather x1, waiting for transfers between devices, on_device(): out_whole = lax.all_gather(frozen_out[0], 'dp', axis=0, tiled=True)  111 us
    all_gather x1, waiting for transfers between devices, on_device(): table_sum = jnp.sum(lax.all_gather(table_part, 'dp'), axis=0)  71.3 us
    dot_general x5, matrix products, contract_last(): lax.dot_general(left, right, (((1,), (1,)), ((), ())), preferred_element_...  22 us
    ppermute x1, waiting for transfers between devices, passed_along(): return lax.ppermute(block, axis, route)  19.7 us
  transfers between devices with their start and end apart: 5, of which 5 were waited for; matrix products, arithmetic and copies ran while one was open for 10% of the time, Pallas kernels for 0%

profile of v1, /device:TPU:24, one launch (start us, length us, event | category | flops | bytes accessed | tf_op | source)
XLA Modules:
  0.0 744.2 jit_solution(3601790440997639089)
XLA Ops:
  7.2 1.5 copy.65
  8.8 1.8 copy.72
  13.9 2.9 copy.62
  17.4 1.5 fusion.92
  18.9 4.2 fusion.93
  23.1 2.3 convolution_convert_fusion
  26.3 1.4 convolution_convert_fusion.3
  27.7 2.0 convolution_add_fusion
  29.8 2.1 copy-done.2
  32.1 1.6 convolution_convert_fusion.4
  33.8 110.7 %all-gather.8.cloned.1.call-done = bf16[1,1536,1536]{2,0,1:T(2,128)(2,1)} async-done(((bf16[1,12,1536]{2,0,1:T(2,128)(2,1)}), bf16[1,1536,1536]{2,0,1:T(2,128)(2,1)}) %all-gather.8.cloned.1.call-update) | async-done | bytes 4718608 | tf_op jit(solution)/shard_map/all_gather | solution.py:93
  144.5 5.5 fusion.5
  149.9 1.5 fusion.51
  151.5 1.4 fusion.7
  152.9 2.2 fusion.11
  155.2 1.4 copy.66
  156.6 2.4 fusion.94
  158.9 7.1 fusion.44
  166.0 6.8 fusion.47
  172.8 2.7 convolution_convert_fusion.1
  177.4 152.7 %all-gather.10.cloned.1.call-done = bf16[1,1536,4608]{2,0,1:T(2,128)(2,1)} async-done(((bf16[1,12,4608]{2,0,1:T(2,128)(2,1)}), bf16[1,1536,4608]{2,0,1:T(2,128)(2,1)}) %all-gather.10.cloned.1.call-update) | async-done | bytes 14155792 | tf_op jit(solution)/shard_map/all_gather | solution.py:122
  330.1 14.4 %fusion.2 = f32[256,1536]{1,0:T(8,128)S(1)} fusion(bf16[1,1536,4608]{2,0,1:T(2,128)(2,1)} %all-gather.10.cloned.1.call-done, bf16[256,1536]{0,1:T(8,128)(2,1)} %bitcast.147, bf16[256,1536]{0,1:T(8,128)(2,1)S(1)} %bitcast.145, bf16[256,1536]{0,1:T(8,128)(2,1)S(1)} %bitcast.142), kind=kOutput, calls=%fused_computation.2 | convolution fusion | flops 3630956544 | bytes 18087936 | tf_op jit(solution)/shard_map/dot_general | solution.py:19
  344.5 2.4 fusion.91
  347.7 2.4 fusion.96
  350.1 2.5 fusion.97
  352.6 3.6 fusion.35
  357.5 4.6 fusion.58
  362.1 6.9 pad_maximum_fusion
  370.1 19.7 %collective-permute-done = bf16[256,1536]{1,0:T(8,128)(2,1)S(1)} collective-permute-done((bf16[256,1536]{1,0:T(8,128)(2,1)S(1)}, bf16[256,1536]{1,0:T(8,128)(2,1)S(1)}, u32[]{:S(2)}, u32[]{:S(2)}) %collective-permute-start) | collective-permute-done | bytes 786464 | tf_op jit(solution)/shard_map/ppermute | solution.py:15
  389.8 71.3 %all-gather.12.cloned.1.call-done = f32[128,3,1536]{2,1,0:T(4,128)} async-done(((f32[1,3,1536]{2,1,0:T(4,128)}), f32[128,3,1536]{2,1,0:T(4,128)}) %all-gather.12.cloned.1.call-update) | async-done | bytes 2359312 | tf_op jit(solution)/shard_map/all_gather | solution.py:148
  461.1 2.4 reduce_sum.109
  464.1 271.3 %reduce-scatter.4.cloned.1.call-done = f32[72,128]{1,0:T(8,128)} async-done(((f32[9216,128]{1,0:T(8,128)}), f32[72,128]{1,0:T(8,128)}) %reduce-scatter.4.cloned.1.call-update) | async-done | bytes 36880
  (71 shorter events, 13.0 us)
Async XLA Ops:
  7.2 20.5 %copy-start = (f32[1,8,4608]{2,1,0:T(8,128)S(1)}, f32[1,8,4608]{2,1,0:T(8,128)}, u32[]{:S(2)}) copy-start(f32[1,8,4608]{2,1,0:T(8,128)} %param.15) | copy-start | bytes 442372
  7.2 137.3 %all-gather.8.cloned.1.call-start = ((), (), s32[]{:S(2)}) async-start(), calls=%async_computation.1 | async-start | bytes 9510912 | tf_op jit(solution)/shard_map/all_gather | solution.py:93
  8.8 321.4 %all-gather.10.cloned.1.call-start = ((), (), s32[]{:S(2)}) async-start(), calls=%async_computation.2 | async-start | bytes 28532736 | tf_op jit(solution)/shard_map/all_gather | solution.py:122
  10.6 450.5 %all-gather.12.cloned.1.call-start = ((), (), s32[]{:S(2)}) async-start(), calls=%async_computation.3 | async-start | bytes 3170304 | tf_op jit(solution)/shard_map/all_gather | solution.py:148
  13.9 2.9 copy-start.3
  18.9 4.2 copy-start.5
  25.4 0.9 copy-start.12
  27.7 4.2 copy-start.4
  29.7 2.2 copy-start.2
  32.1 119.3 %copy-start.9 = (bf16[256,1536]{1,0:T(8,128)(2,1)}, bf16[256,1536]{1,0:T(8,128)(2,1)S(1)}, u32[]{:S(2)}) copy-start(bf16[256,1536]{1,0:T(8,128)(2,1)S(1)} %fusion.37) | copy-start | bytes 2359300
  144.5 7.0 copy-start.14
  158.9 7.1 copy-start.10
  172.8 3.6 copy-start.13
  172.8 3.6 copy-start.15
  172.8 3.6 copy-start.16
  175.5 0.9 copy-start.18
  176.4 153.7 %copy-start.17 = (bf16[12,256,128]{1,2,0:T(8,128)(2,1)S(1)}, bf16[12,256,128]{1,2,0:T(8,128)(2,1)}, u32[]{:S(2)}) copy-start(bf16[12,256,128]{1,2,0:T(8,128)(2,1)} %fusion.47) | copy-start | bytes 2359300
  347.6 387.7 %reduce-scatter.4.cloned.1.call-start = ((), (), s32[]{:S(2)}) async-start(), calls=%async_computation.4 | async-start | bytes 4755456
  356.1 0.9 copy-start.8
  357.4 4.7 copy-start.6
  357.4 4.7 copy-start.7
  369.0 1.1 copy-start.11
  370.1 19.7 %collective-permute-start = (bf16[256,1536]{1,0:T(8,128)(2,1)S(1)}, bf16[256,1536]{1,0:T(8,128)(2,1)S(1)}, u32[]{:S(2)}, u32[]{:S(2)}) collective-permute-start(bf16[256,1536]{1,0:T(8,128)(2,1)S(1)} %copy-done.11), channel_id=1, source_target_pairs={{1,0},{0,1},{3,2},{2,3},{5,4},{4,5},{7,6},{6,7},{9,8},{8,9},{11,10... | collective-permute-start | bytes 2359304 | tf_op jit(solution)/shard_map/ppermute | solution.py:15
  389.8 347.8 %copy-start.1 = (f32[1,8,4608]{2,1,0:T(8,128)S(1)}, f32[1,8,4608]{2,1,0:T(8,128)}, u32[]{:S(2)}) copy-start(f32[1,8,4608]{2,1,0:T(8,128)} %param.15) | copy-start | bytes 442372
Sparse Core Ops, SparseCore 0:
  11.9 132.5 all-gather.7
  148.3 181.7 all-gather.9
  347.8 113.2 all-gather.11
  466.9 268.4 reduce-scatter.3
